TPU v7x, 256 devices: a whole 4x4x8 slice. The times are simulated.
256 devices in a mesh: dom: 64 (over y, z, core), mp: 4 (over x).
Axes of the slice: x: 4, y: 4, z: 8, core: 2. Of those that a mesh axis runs over, the one named last changes fastest.
Arguments:
- vertex_embedding: bfloat16 [32768, 512], P('dom'), may hold values from -6 to 6
- prenorm_mixer_scale: float32 [512], replicated, may hold values from 0.25 to 1.75
- prenorm_perceptron_scale: float32 [512], replicated, may hold values from 0.25 to 1.75
- triple_projector_stack: bfloat16 [3, 512, 512], P(None, None, 'mp'), may hold values from -0.25 to 0.25
- channel_logit_scaling: float32 [8], P('mp'), may hold values from 0.06 to 8
- mixer_final_projector: bfloat16 [512, 512], P('mp'), may hold values from -0.25 to 0.25
- neighbour_mixer_projector: bfloat16 [512, 512], P('mp'), may hold values from -0.25 to 0.25
- expand_projector: bfloat16 [512, 2048], P(None, 'mp'), may hold values from -0.25 to 0.25
- contract_projector: bfloat16 [2048, 512], P('mp'), may hold values from -0.125 to 0.125
- matched_companion: int32 [2, 64], replicated, may hold values from 0 to 63, as said below
- boundary_sender_vertex: int32 [64, 64, 128], P('dom'), may hold values from 0 to 511
- boundary_slot_tally: int32 [64, 64], P('dom'), may hold values from 0 to 128, as said below
- boundary_landing_vertex: int32 [64, 64, 128], P('dom'), may hold values from 0 to 511
- partition_edge_tail: int32 [64, 16384], P('dom'), may hold values from 0 to 511
- partition_edge_sink: int32 [64, 16384], P('dom'), may hold values from 0 to 511
Outputs:
- updated: bfloat16 [32768, 512], P(('dom', 'mp'))
Inputs may be any that keep to these rules, and one draw needn't show every extreme that they name: matched_companion[j, b] equals b XOR c_j for one number c_j of each matching; c_0 and c_1 are at least 1 and differ. Slots at and beyond boundary_slot_tally[s, d] of the 128 slots from s to d are unused; the diagonal is 0; the largest entry is 128.
All inputs are finite; a program needn't handle non-finite values.
Results may differ from a plain program's by a relative error of at most 0.012.
The roundings to bfloat16 on the way count: a program that leaves them out, or rounds other values in their place, can miss the bound.
Values may be sent and summed in bfloat16 or wider, within the bound.
A program may use at most 64 MiB of HBM per device.

v0:
```python
import math

import jax
import jax.numpy as jnp
from jax import lax
from jax.sharding import PartitionSpec as P

HEAD_SIZE = 64
BLOCK_NODES = 512
CAP = 128


epsilon = 1e-05


def swapped(block, axis, bit):
    count = lax.axis_size(axis)
    route = []
    for low in range(count):
        high = low | 1 << bit
        if high != low and high < count:
            route += [(low, high), (high, low)]
    return lax.ppermute(block, axis, route)


def cut_along(value, dim, size):
    shape = value.shape
    tiles = value.reshape(*shape[:dim], size, shape[dim] // size, *shape[dim + 1 :])
    return jnp.moveaxis(tiles, dim, 0)


def sum_at_owner(value, axis, dim):
    size = lax.axis_size(axis)
    tiles = lax.all_to_all(cut_along(value, dim, size), axis, 0, 0, tiled=True)
    return jnp.sum(tiles.astype(jnp.float32), axis=0)


def normalize(matrix, scale_gain):
    matrix = matrix.astype(jnp.float32)
    row_mean = jnp.mean(matrix, -1, keepdims=True)
    centred = matrix - row_mean
    variance = jnp.mean(centred * centred, -1, keepdims=True)
    return (centred * lax.rsqrt(variance + epsilon) * scale_gain).astype(jnp.bfloat16)


def tile_softmax_mixing(asking_vertices, lookup_tensor, content_tensor, channel_logit_scaling):
    affinity_table = jnp.einsum(
        "rhd,shd->hrs", asking_vertices, lookup_tensor, preferred_element_type=jnp.float32
    )
    affinity_table = affinity_table * channel_logit_scaling[:, None, None]
    weights = jax.nn.softmax(affinity_table, axis=-1).astype(jnp.bfloat16)
    attended = jnp.einsum(
        "hrs,shd->rhd", weights, content_tensor, preferred_element_type=jnp.float32
    )
    return attended.astype(jnp.bfloat16)


def route_copy(routed, mask_value):
    for bit_number in range(lax.axis_size("dom").bit_length() - 1):
        needed = jnp.bitwise_and(jnp.right_shift(mask_value, bit_number), 1) == 1
        routed = lax.cond(
            needed,
            lambda carried: swapped(carried, "dom", bit_number),
            lambda carried: carried,
            routed,
        )
    return routed


def land_rows(values, targets, flags, node_rows):
    total = targets.shape[0]
    feature_width = values.shape[1]
    step_rows = math.gcd(total, 2048)
    turns = total // step_rows
    columns = jnp.arange(node_rows, dtype=jnp.int32)

    def accumulate(carry, inputs):
        sums, counts = carry
        part_values, part_targets, part_flags = inputs
        selector = (part_targets[:, None] == columns[None, :]).astype(jnp.bfloat16)
        sums = sums + jnp.einsum(
            "mr,mw->rw", selector, part_values, preferred_element_type=jnp.float32
        )
        counts = counts + jnp.dot(part_flags, selector, preferred_element_type=jnp.float32)
        return ((sums, counts), None)

    initial = (
        jnp.zeros((node_rows, feature_width), jnp.float32),
        jnp.zeros((node_rows,), jnp.float32),
    )
    (sums, counts), unused = lax.scan(
        accumulate,
        initial,
        (
            values.reshape(turns, step_rows, feature_width),
            targets.reshape(turns, step_rows),
            flags.reshape(turns, step_rows),
        ),
    )
    return (sums, counts)


def body(
    vertex_embedding,
    prenorm_mixer_scale,
    prenorm_perceptron_scale,
    triple_projector_stack,
    channel_logit_scaling,
    mixer_final_projector,
    neighbour_mixer_projector,
    expand_projector,
    contract_projector,
    matched_companion,
    boundary_sender_vertex,
    boundary_slot_tally,
    boundary_landing_vertex,
    partition_edge_tail,
    partition_edge_sink,
):
    node_dev = vertex_embedding.shape[0]
    blocks = node_dev // BLOCK_NODES
    partition_channel_split = channel_logit_scaling.shape[0]
    width_here = partition_channel_split * HEAD_SIZE
    normed = normalize(vertex_embedding, prenorm_mixer_scale)
    projected = jnp.einsum(
        "nd,tdc->tnc", normed, triple_projector_stack, preferred_element_type=jnp.float32
    ).astype(jnp.bfloat16)
    asking_vertices = projected[0]
    key_value = jnp.concatenate([projected[1], projected[2]], axis=1)
    mask_pair = matched_companion[:, 0]
    device_mask = mask_pair // blocks
    local_mask = mask_pair % blocks
    routed_one = route_copy(key_value, device_mask[0])
    routed_two = route_copy(key_value, device_mask[1])
    block_order = jnp.arange(blocks, dtype=jnp.int32)
    fetched_one = routed_one.reshape(blocks, BLOCK_NODES, 2 * width_here)[
        jnp.bitwise_xor(block_order, local_mask[0])
    ]
    fetched_two = routed_two.reshape(blocks, BLOCK_NODES, 2 * width_here)[
        jnp.bitwise_xor(block_order, local_mask[1])
    ]
    own_pairs = key_value.reshape(blocks, BLOCK_NODES, 2 * width_here)
    all_pairs = jnp.concatenate([own_pairs, fetched_one, fetched_two], axis=1)

    def per_block(inputs):
        block_queries, pair_block = inputs
        block_keys = pair_block[:, :width_here].reshape(
            3 * BLOCK_NODES, partition_channel_split, HEAD_SIZE
        )
        block_values = pair_block[:, width_here:].reshape(
            3 * BLOCK_NODES, partition_channel_split, HEAD_SIZE
        )
        return tile_softmax_mixing(
            block_queries.reshape(BLOCK_NODES, partition_channel_split, HEAD_SIZE),
            block_keys,
            block_values,
            channel_logit_scaling,
        )

    attended = lax.map(
        per_block, (asking_vertices.reshape(blocks, BLOCK_NODES, width_here), all_pairs)
    ).reshape(node_dev, width_here)
    attn_term = jnp.dot(attended, mixer_final_projector, preferred_element_type=jnp.float32)
    mp_index = lax.axis_index("mp")
    width_q = neighbour_mixer_projector.shape[0]
    quarter = lax.dynamic_slice_in_dim(vertex_embedding, mp_index * width_q, width_q, 1)
    slot_index = jnp.arange(CAP, dtype=jnp.int32)
    live_slots = slot_index[None, :] < boundary_slot_tally[0][:, None]
    outgoing = jnp.where(
        live_slots[..., None], quarter[boundary_sender_vertex[0]], jnp.zeros((), jnp.bfloat16)
    )
    incoming, arrived = (
        lax.all_to_all(outgoing, "dom", split_axis=0, concat_axis=0, tiled=True),
        lax.all_to_all(
            live_slots.astype(jnp.bfloat16), "dom", split_axis=0, concat_axis=0, tiled=True
        ),
    )
    targets = boundary_landing_vertex[0].reshape(-1)
    boundary, degree = land_rows(
        incoming.reshape(-1, width_q), targets, arrived.reshape(-1), node_dev
    )
    edge_count = partition_edge_sink.shape[1]
    local_sum, local_degree = land_rows(
        quarter[partition_edge_tail[0]],
        partition_edge_sink[0],
        jnp.ones((edge_count,), jnp.bfloat16),
        node_dev,
    )
    degree = degree + local_degree
    message = (
        (quarter.astype(jnp.float32) + local_sum + boundary) / (1.0 + degree)[:, None]
    ).astype(jnp.bfloat16)
    partial_terms = attn_term + jnp.dot(
        message, neighbour_mixer_projector, preferred_element_type=jnp.float32
    )
    share_rows = node_dev // lax.axis_size("mp")
    summed = sum_at_owner(partial_terms.astype(jnp.bfloat16), "mp", 0)
    own_rows = lax.dynamic_slice_in_dim(vertex_embedding, mp_index * share_rows, share_rows, 0)
    mixed_share = own_rows.astype(jnp.float32) + summed
    normed_share = normalize(mixed_share, prenorm_perceptron_scale)
    hidden = jax.nn.gelu(
        jnp.dot(
            lax.all_gather(normed_share, "mp", axis=0, tiled=True),
            expand_projector,
            preferred_element_type=jnp.float32,
        ),
        approximate=False,
    ).astype(jnp.bfloat16)
    down_share = sum_at_owner(
        jnp.dot(hidden, contract_projector, preferred_element_type=jnp.float32).astype(
            jnp.bfloat16
        ),
        "mp",
        0,
    )
    return (mixed_share + down_share).astype(jnp.bfloat16)


def solution(mesh):
    return jax.shard_map(
        body,
        mesh=mesh,
        in_specs=(
            P("dom", None),
            P(),
            P(),
            P(None, None, "mp"),
            P("mp"),
            P("mp", None),
            P("mp", None),
            P(None, "mp"),
            P("mp", None),
            P(),
            P("dom", None, None),
            P("dom", None),
            P("dom", None, None),
            P("dom", None),
            P("dom", None),
        ),
        out_specs=P(("dom", "mp"), None),
        check_vma=False,
    )
```

profile of v0, /device:TPU:1, one launch (start us, length us, event | category | flops | bytes accessed | tf_op | source)
XLA Modules:
  0.0 315.5 jit_solution(13903787879440678558)
XLA Ops:
  0.0 1.5 compare_convert_fusion
  1.5 13.2 %all-to-all-start.1 = ((bf16[64,1,128]{2,1,0:T(2,128)(2,1)}), bf16[64,1,128]{2,1,0:T(2,128)(2,1)S(1)}, u32[]{:S(2)}, u32[]{:S(2)}) async-start(bf16[64,1,128]{2,1,0:T(2,128)(2,1)} %compare_convert_fusion), calls=%async_computation.1 | async-start | bytes 65536 | tf_op jit(solution)/shard_map/all_to_all | solution.py:174
  27.5 1.6 fusion.51
  29.4 1.9 conditional.18
  32.0 8.4 %conditional.19 = (bf16[512,256]{1,0:T(8,128)(2,1)}) conditional(s32[]{:T(128)} %bitcast.21, bf16[512,256]{1,0:T(8,128)(2,1)} %get-tuple-element.369, bf16[512,256]{1,0:T(8,128)(2,1)} %get-tuple-element.369), branch_computations={%region_16.17_spmd, %region_17.18_spmd} | conditional | bytes 1572912 | solution.py:61
  33.3 6.4 %collective-permute-done.7 = bf16[512,256]{1,0:T(8,128)(2,1)S(1)} collective-permute-done((bf16[512,256]{1,0:T(8,128)(2,1)}, bf16[512,256]{1,0:T(8,128)(2,1)S(1)}, u32[]{:S(2)}, u32[]{:S(2)}) %collective-permute-start.7) | collective-permute-done | bytes 262176 | tf_op jit(solution)/shard_map/cond/branch_1_fun/ppermute | solution.py:23
  40.4 13.3 %conditional.21 = (bf16[512,256]{1,0:T(8,128)(2,1)}) conditional(s32[]{:T(128)} %bitcast.19, bf16[512,256]{1,0:T(8,128)(2,1)} %get-tuple-element.371, bf16[512,256]{1,0:T(8,128)(2,1)} %get-tuple-element.371), branch_computations={%region_20.21_spmd, %region_21.22_spmd} | conditional | bytes 1572912 | solution.py:61
  40.4 5.2 %collective-permute-start.9 = (bf16[512,256]{1,0:T(8,128)(2,1)}, bf16[512,256]{1,0:T(8,128)(2,1)S(1)}, u32[]{:S(2)}, u32[]{:S(2)}) collective-permute-start(bf16[512,256]{1,0:T(8,128)(2,1)} %param.19), channel_id=1, source_target_pairs={{0,32},{32,0},{4,36},{36,4},{8,40},{40,8},{12,44},{44,12},{16,48},... | collective-permute-start | bytes 786440 | tf_op jit(solution)/shard_map/cond/branch_1_fun/ppermute | solution.py:23
  45.6 7.4 %collective-permute-done.9 = bf16[512,256]{1,0:T(8,128)(2,1)S(1)} collective-permute-done((bf16[512,256]{1,0:T(8,128)(2,1)}, bf16[512,256]{1,0:T(8,128)(2,1)S(1)}, u32[]{:S(2)}, u32[]{:S(2)}) %collective-permute-start.9) | collective-permute-done | bytes 262176 | tf_op jit(solution)/shard_map/cond/branch_1_fun/ppermute | solution.py:23
  53.7 6.4 %conditional.22 = (bf16[512,256]{1,0:T(8,128)(2,1)}) conditional(s32[]{:T(128)} %bitcast.18, bf16[512,256]{1,0:T(8,128)(2,1)} %get-tuple-element.372, bf16[512,256]{1,0:T(8,128)(2,1)} %get-tuple-element.372), branch_computations={%region_22.23_spmd, %region_23.24_spmd} | conditional | bytes 1572912 | solution.py:61
  55.0 4.4 %collective-permute-done.10 = bf16[512,256]{1,0:T(8,128)(2,1)S(1)} collective-permute-done((bf16[512,256]{1,0:T(8,128)(2,1)}, bf16[512,256]{1,0:T(8,128)(2,1)S(1)}, u32[]{:S(2)}, u32[]{:S(2)}) %collective-permute-start.10) | collective-permute-done | bytes 262176 | tf_op jit(solution)/shard_map/cond/branch_1_fun/ppermute | solution.py:23
  60.1 7.2 %conditional.23 = (bf16[1,512,256]{1,2,0:T(8,128)(2,1)S(1)}) conditional(s32[]{:T(128)} %bitcast.17, bf16[512,256]{1,0:T(8,128)(2,1)} %get-tuple-element.373, bf16[512,256]{1,0:T(8,128)(2,1)} %get-tuple-element.373), branch_computations={%region_24.25_spmd, %region_25.26_spmd} | conditional | bytes 1572912 | solution.py:61
  60.1 2.9 collective-permute-start.11
  63.1 4.1 %collective-permute-done.11 = bf16[512,256]{1,0:T(8,128)(2,1)S(1)} collective-permute-done((bf16[512,256]{1,0:T(8,128)(2,1)}, bf16[512,256]{1,0:T(8,128)(2,1)S(1)}, u32[]{:S(2)}, u32[]{:S(2)}) %collective-permute-start.11) | collective-permute-done | bytes 262176 | tf_op jit(solution)/shard_map/cond/branch_1_fun/ppermute | solution.py:23
  67.3 9.5 %conditional.13 = (bf16[512,256]{1,0:T(8,128)(2,1)}) conditional(s32[]{:T(128)} %bitcast.15, bf16[512,256]{1,0:T(8,128)(2,1)} %get-tuple-element.364, bf16[512,256]{1,0:T(8,128)(2,1)} %get-tuple-element.364), branch_computations={%region_4.5_spmd, %region_5.6_spmd} | conditional | bytes 1572912 | solution.py:61
  67.4 4.8 %collective-permute-start.1 = (bf16[512,256]{1,0:T(8,128)(2,1)}, bf16[512,256]{1,0:T(8,128)(2,1)S(1)}, u32[]{:S(2)}, u32[]{:S(2)}) collective-permute-start(bf16[512,256]{1,0:T(8,128)(2,1)} %param.3), channel_id=1, source_target_pairs={{0,8},{8,0},{4,12},{12,4},{16,24},{24,16},{20,28},{28,20},{32,40},... | collective-permute-start | bytes 786440 | tf_op jit(solution)/shard_map/cond/branch_1_fun/ppermute | solution.py:23
  72.1 4.0 %collective-permute-done.1 = bf16[512,256]{1,0:T(8,128)(2,1)S(1)} collective-permute-done((bf16[512,256]{1,0:T(8,128)(2,1)}, bf16[512,256]{1,0:T(8,128)(2,1)S(1)}, u32[]{:S(2)}, u32[]{:S(2)}) %collective-permute-start.1) | collective-permute-done | bytes 262176 | tf_op jit(solution)/shard_map/cond/branch_1_fun/ppermute | solution.py:23
  76.8 19.3 %conditional.14 = (bf16[512,256]{1,0:T(8,128)(2,1)}) conditional(s32[]{:T(128)} %bitcast.14, bf16[512,256]{1,0:T(8,128)(2,1)} %get-tuple-element.365, bf16[512,256]{1,0:T(8,128)(2,1)} %get-tuple-element.365), branch_computations={%region_6.7_spmd, %region_7.8_spmd} | conditional | bytes 1572912 | solution.py:61
  76.8 6.8 %collective-permute-start.2 = (bf16[512,256]{1,0:T(8,128)(2,1)}, bf16[512,256]{1,0:T(8,128)(2,1)S(1)}, u32[]{:S(2)}, u32[]{:S(2)}) collective-permute-start(bf16[512,256]{1,0:T(8,128)(2,1)} %param.5), channel_id=1, source_target_pairs={{0,16},{16,0},{4,20},{20,4},{8,24},{24,8},{12,28},{28,12},{32,48},... | collective-permute-start | bytes 786440 | tf_op jit(solution)/shard_map/cond/branch_1_fun/ppermute | solution.py:23
  83.6 11.8 %collective-permute-done.2 = bf16[512,256]{1,0:T(8,128)(2,1)S(1)} collective-permute-done((bf16[512,256]{1,0:T(8,128)(2,1)}, bf16[512,256]{1,0:T(8,128)(2,1)S(1)}, u32[]{:S(2)}, u32[]{:S(2)}) %collective-permute-start.2) | collective-permute-done | bytes 262176 | tf_op jit(solution)/shard_map/cond/branch_1_fun/ppermute | solution.py:23
  96.1 8.7 %conditional.17 = (bf16[1,512,256]{1,2,0:T(8,128)(2,1)S(1)}) conditional(s32[]{:T(128)} %bitcast.11, bf16[512,256]{1,0:T(8,128)(2,1)} %get-tuple-element.368, bf16[512,256]{1,0:T(8,128)(2,1)} %get-tuple-element.368), branch_computations={%region_12.13_spmd, %region_13.14_spmd} | conditional | bytes 1572912 | solution.py:61
  96.1 3.1 collective-permute-start.5
  99.2 5.3 %collective-permute-done.5 = bf16[512,256]{1,0:T(8,128)(2,1)S(1)} collective-permute-done((bf16[512,256]{1,0:T(8,128)(2,1)}, bf16[512,256]{1,0:T(8,128)(2,1)S(1)}, u32[]{:S(2)}, u32[]{:S(2)}) %collective-permute-start.5) | collective-permute-done | bytes 262176 | tf_op jit(solution)/shard_map/cond/branch_1_fun/ppermute | solution.py:23
  106.1 24.0 %gather_fusion.1 = bf16[8192,128]{1,0:T(8,128)(2,1)S(1)} fusion(bf16[512,128]{1,0:T(8,128)(2,1)S(1)} %constant_dynamic-slice_fusion.2, s32[8192]{0:T(1024)S(1)} %fusion.88), kind=kCustom, calls=%fused_computation.1 | custom fusion | bytes 4227072 | tf_op jit(solution)/shard_map/gather | solution.py:170
  130.2 2.7 broadcast_select_fusion
  132.9 5.5 %fusion.124 = (f32[2,512]{1,0:T(2,128)S(1)}, f32[2,512,1536]{2,1,0:T(8,128)}) fusion(f32[2]{0:T(128)S(1)} %copy-done.10, bf16[512,2,64]{0,2,1:T(8,128)(2,1)S(1)} %bitcast.106, bf16[1536,2,64]{0,2,1:T(8,128)(2,1)} %bitcast.97), kind=kOutput, calls=%fused_computation.165 | convolution fusion | flops 206046720 | bytes 6819848 | tf_op jit(solution)/shard_map/while/body/eval_jaxpr/sub | solution.py:51
  138.4 4.0 %fusion.34 = bf16[2,64,512]{2,1,0:T(8,128)(2,1)S(1)} fusion(bf16[1536,2,64]{0,2,1:T(8,128)(2,1)S(1)} %bitcast.96, f32[2,512,1536]{2,1,0:T(8,128)} %get-tuple-element.246, f32[2,512]{1,0:T(2,128)S(1)} %get-tuple-element.245), kind=kOutput, calls=%fused_computation.47 | convolution fusion | flops 204537856 | bytes 6819840 | tf_op jit(solution)/shard_map/while/body/eval_jaxpr/hrs,shd->rhd/dot_general | solution.py:52
  144.2 57.8 %gather_fusion = bf16[16384,128]{1,0:T(8,128)(2,1)} fusion(bf16[512,128]{1,0:T(8,128)(2,1)S(1)} %constant_dynamic-slice_fusion.2, s32[16384]{0:T(1024)S(1)} %broadcast_clamp_fusion), kind=kCustom, calls=%fused_computation | custom fusion | bytes 8454144 | tf_op jit(solution)/shard_map/gather | solution.py:184
  202.0 9.7 %all-to-all-start = ((bf16[64,128,128]{2,1,0:T(8,128)(2,1)}), bf16[64,128,128]{2,1,0:T(8,128)(2,1)}, u32[]{:S(2)}, u32[]{:S(2)}) async-start(bf16[64,128,128]{2,1,0:T(8,128)(2,1)} %broadcast_select_fusion), calls=%async_computation | async-start | bytes 4194304 | tf_op jit(solution)/shard_map/all_to_all | solution.py:173
  211.6 27.8 %while.30 = (s32[]{:T(128)}, f32[512,128]{1,0:T(8,128)S(1)}, f32[512]{0:T(512)S(1)}, s32[8,2048]{1,0:T(8,128)S(1)}, bf16[8,2048,128]{2,1,0:T(8,128)(2,1)}, /*index=5*/s32[]{:T(128)}, s32[]{:T(128)}) while((s32[]{:T(128)}, f32[512,128]{1,0:T(8,128)S(1)}, f32[512]{0:T(512)S(1)}, s32[8,2048]{1,0:T(8,128)S(1)}, ...), condition=%wide.region_29.30_spmd.clone, body=%wide.region_28.29_spmd.clone.sunk | while | flops 272761856 | bytes 1089640 | solution.py:91
  211.7 2.6 fusion.150
  215.2 2.6 fusion.150
  218.6 2.6 fusion.150
  222.1 2.6 fusion.150
  225.6 2.6 fusion.150
  229.1 2.6 fusion.150
  232.5 2.6 fusion.150
  236.0 2.6 fusion.150
  239.6 23.2 %all-to-all-done = bf16[64,128,128]{2,1,0:T(8,128)(2,1)} async-done(((bf16[64,128,128]{2,1,0:T(8,128)(2,1)}), bf16[64,128,128]{2,1,0:T(8,128)(2,1)}, u32[]{:S(2)}, u32[]{:S(2)}) %all-to-all-start) | async-done | bytes 2097184 | tf_op jit(solution)/shard_map/all_to_all | solution.py:173
  262.8 14.0 %while.31 = (s32[]{:T(128)}, f32[512,128]{1,0:T(8,128)S(1)}, f32[512]{0:T(512)S(1)}, s32[4,2048]{1,0:T(4,128)S(1)}, bf16[4,2048,128]{2,1,0:T(8,128)(2,1)}, /*ind...) while((s32[]{:T(128)}, f32[512,128]{1,0:T(8,128)S(1)}, f32[512]{0:T(512)S(1)}, ...), condition=%wide.region_31.32_spmd.clone, body=%wide.region_30.31_spmd.clone.sunk | while | flops 272761856 | bytes 1097844 | solution.py:91
  262.8 2.7 fusion.154
  266.3 2.6 fusion.154
  269.8 2.6 fusion.154
  273.3 2.6 fusion.154
  277.2 12.4 %all_to_all.21 = bf16[4,128,512]{2,1,0:T(8,128)(2,1)S(1)} all-to-all(bf16[4,128,512]{2,1,0:T(8,128)(2,1)S(1)} %bitcast.92), channel_id=1, replica_groups=mesh['dom'=64,'mp'=4] {'mp'}, dimensions={0} | all-to-all | bytes 1048576 | tf_op jit(solution)/shard_map/all_to_all | solution.py:34
  290.1 11.3 %all_gather.3 = bf16[512,512]{1,0:T(8,128)(2,1)S(1)} all-gather(bf16[128,512]{1,0:T(8,128)(2,1)S(1)} %multiply_convert_fusion), channel_id=1, replica_groups=mesh['dom'=64,'mp'=4] {'mp'}, dimensions={0}, use_global_device_ids=true | all-gather | bytes 655360 | tf_op jit(solution)/shard_map/all_gather | solution.py:203
  301.4 3.9 %convolution_convert_fusion = bf16[512,512]{1,0:T(8,128)(2,1)S(1)} fusion(bf16[512,512]{1,0:T(8,128)(2,1)S(1)} %copy-done, bf16[512,512]{1,0:T(8,128)(2,1)S(1)} %all_gather.3, bf16[512,512]{1,0:T(8,128)(2,1)} %param.50), kind=kOutput, calls=%fused_computation.44 | convolution fusion | flops 554172416 | bytes 2097152 | tf_op jit(solution)/shard_map/dot_general | solution.py:210
  305.3 9.3 %all_to_all.22 = bf16[4,128,512]{2,1,0:T(8,128)(2,1)S(1)} all-to-all(bf16[4,128,512]{2,1,0:T(8,128)(2,1)S(1)} %bitcast.94), channel_id=1, replica_groups=mesh['dom'=64,'mp'=4] {'mp'}, dimensions={0} | all-to-all | bytes 1048576 | tf_op jit(solution)/shard_map/all_to_all | solution.py:34
  (113 shorter events, 30.0 us)
Async XLA Ops:
  0.0 301.4 %copy-start = (bf16[512,512]{1,0:T(8,128)(2,1)S(1)}, bf16[512,512]{1,0:T(8,128)(2,1)}, u32[]{:S(2)}) copy-start(bf16[512,512]{1,0:T(8,128)(2,1)} %param.51) | copy-start | bytes 1572868
  1.5 200.5 %all-to-all-start.1 = ((bf16[64,1,128]{2,1,0:T(2,128)(2,1)}), bf16[64,1,128]{2,1,0:T(2,128)(2,1)S(1)}, u32[]{:S(2)}, u32[]{:S(2)}) async-start(bf16[64,1,128]{2,1,0:T(2,128)(2,1)} %compare_convert_fusion), calls=%async_computation.1 | async-start | bytes 65536 | tf_op jit(solution)/shard_map/all_to_all | solution.py:174
  29.4 1.8 collective-permute-start.6
  32.0 7.7 %collective-permute-start.7 = (bf16[512,256]{1,0:T(8,128)(2,1)}, bf16[512,256]{1,0:T(8,128)(2,1)S(1)}, u32[]{:S(2)}, u32[]{:S(2)}) collective-permute-start(bf16[512,256]{1,0:T(8,128)(2,1)} %param.15), channel_id=1, source_target_pairs={{0,8},{8,0},{4,12},{12,4},{16,24},{24,16},{20,28},{28,20},{32,40},... | collective-permute-start | bytes 786440 | tf_op jit(solution)/shard_map/cond/branch_1_fun/ppermute | solution.py:23
  40.4 65.6 %copy-start.1 = (bf16[512,512]{1,0:T(8,128)(2,1)S(1)}, bf16[512,512]{1,0:T(8,128)(2,1)}, u32[]{:S(2)}) copy-start(bf16[512,512]{1,0:T(8,128)(2,1)} %param.43) | copy-start | bytes 1572868
  40.4 12.6 %collective-permute-start.9 = (bf16[512,256]{1,0:T(8,128)(2,1)}, bf16[512,256]{1,0:T(8,128)(2,1)S(1)}, u32[]{:S(2)}, u32[]{:S(2)}) collective-permute-start(bf16[512,256]{1,0:T(8,128)(2,1)} %param.19), channel_id=1, source_target_pairs={{0,32},{32,0},{4,36},{36,4},{8,40},{40,8},{12,44},{44,12},{16,48},... | collective-permute-start | bytes 786440 | tf_op jit(solution)/shard_map/cond/branch_1_fun/ppermute | solution.py:23
  53.7 52.3 %copy-start.7 = (s32[1,64,128]{2,1,0:T(8,128)S(1)}, s32[1,64,128]{2,1,0:T(8,128)}, u32[]{:S(2)}) copy-start(s32[1,64,128]{2,1,0:T(8,128)} %param.53) | copy-start | bytes 98308
  53.7 52.3 %copy-start.5 = (s32[1,16384]{1,0:T(1,128)S(1)}, s32[1,16384]{1,0:T(1,128)}, u32[]{:S(2)}) copy-start(s32[1,16384]{1,0:T(1,128)} %param.56) | copy-start | bytes 196612
  53.7 5.7 %collective-permute-start.10 = (bf16[512,256]{1,0:T(8,128)(2,1)}, bf16[512,256]{1,0:T(8,128)(2,1)S(1)}, u32[]{:S(2)}, u32[]{:S(2)}) collective-permute-start(bf16[512,256]{1,0:T(8,128)(2,1)} %param.21), channel_id=1, source_target_pairs={{0,64},{64,0},{4,68},{68,4},{8,72},{72,8},{12,76},{76,12},{16,80},... | collective-permute-start | bytes 786440 | tf_op jit(solution)/shard_map/cond/branch_1_fun/ppermute | solution.py:23
  60.1 7.0 %collective-permute-start.11 = (bf16[512,256]{1,0:T(8,128)(2,1)}, bf16[512,256]{1,0:T(8,128)(2,1)S(1)}, u32[]{:S(2)}, u32[]{:S(2)}) collective-permute-start(bf16[512,256]{1,0:T(8,128)(2,1)} %param.23), channel_id=1, source_target_pairs={{0,128},{128,0},{4,132},{132,4},{8,136},{136,8},{12,140},{140,12},... | collective-permute-start | bytes 786440 | tf_op jit(solution)/shard_map/cond/branch_1_fun/ppermute | solution.py:23
  67.4 8.8 %collective-permute-start.1 = (bf16[512,256]{1,0:T(8,128)(2,1)}, bf16[512,256]{1,0:T(8,128)(2,1)S(1)}, u32[]{:S(2)}, u32[]{:S(2)}) collective-permute-start(bf16[512,256]{1,0:T(8,128)(2,1)} %param.3), channel_id=1, source_target_pairs={{0,8},{8,0},{4,12},{12,4},{16,24},{24,16},{20,28},{28,20},{32,40},... | collective-permute-start | bytes 786440 | tf_op jit(solution)/shard_map/cond/branch_1_fun/ppermute | solution.py:23
  76.8 18.6 %collective-permute-start.2 = (bf16[512,256]{1,0:T(8,128)(2,1)}, bf16[512,256]{1,0:T(8,128)(2,1)S(1)}, u32[]{:S(2)}, u32[]{:S(2)}) collective-permute-start(bf16[512,256]{1,0:T(8,128)(2,1)} %param.5), channel_id=1, source_target_pairs={{0,16},{16,0},{4,20},{20,4},{8,24},{24,8},{12,28},{28,12},{32,48},... | collective-permute-start | bytes 786440 | tf_op jit(solution)/shard_map/cond/branch_1_fun/ppermute | solution.py:23
  96.1 8.4 %collective-permute-start.5 = (bf16[512,256]{1,0:T(8,128)(2,1)}, bf16[512,256]{1,0:T(8,128)(2,1)S(1)}, u32[]{:S(2)}, u32[]{:S(2)}) collective-permute-start(bf16[512,256]{1,0:T(8,128)(2,1)} %param.11), channel_id=1, source_target_pairs={{0,128},{128,0},{4,132},{132,4},{8,136},{136,8},{12,140},{140,12},... | collective-permute-start | bytes 786440 | tf_op jit(solution)/shard_map/cond/branch_1_fun/ppermute | solution.py:23
  130.1 2.7 copy-start.10
  132.9 5.6 %copy-start.2 = (bf16[1536,128]{0,1:T(8,128)(2,1)S(1)}, bf16[1536,128]{0,1:T(8,128)(2,1)}, u32[]{:S(2)}) copy-start(bf16[1536,128]{0,1:T(8,128)(2,1)} %get-tuple-element.237) | copy-start | bytes 1179652
  138.4 4.0 %copy-start.3 = (bf16[128,512]{1,0:T(8,128)(2,1)S(1)}, bf16[128,512]{1,0:T(8,128)(2,1)}, u32[]{:S(2)}) copy-start(bf16[128,512]{1,0:T(8,128)(2,1)} %param.48) | copy-start | bytes 393220
  138.4 4.4 %copy-start.8 = (s32[1,64,128]{2,1,0:T(8,128)S(1)}, s32[1,64,128]{2,1,0:T(8,128)}, u32[]{:S(2)}) copy-start(s32[1,64,128]{2,1,0:T(8,128)} %param.55) | copy-start | bytes 98308
  138.4 4.9 %copy-start.6 = (s32[1,16384]{1,0:T(1,128)S(1)}, s32[1,16384]{1,0:T(1,128)}, u32[]{:S(2)}) copy-start(s32[1,16384]{1,0:T(1,128)} %param.57) | copy-start | bytes 196612
  202.0 60.8 %all-to-all-start = ((bf16[64,128,128]{2,1,0:T(8,128)(2,1)}), bf16[64,128,128]{2,1,0:T(8,128)(2,1)}, u32[]{:S(2)}, u32[]{:S(2)}) async-start(bf16[64,128,128]{2,1,0:T(8,128)(2,1)} %broadcast_select_fusion), calls=%async_computation | async-start | bytes 4194304 | tf_op jit(solution)/shard_map/all_to_all | solution.py:173
  262.8 14.0 %copy-start.4 = (bf16[128,512]{1,0:T(8,128)(2,1)S(1)}, bf16[128,512]{1,0:T(8,128)(2,1)}, u32[]{:S(2)}) copy-start(bf16[128,512]{1,0:T(8,128)(2,1)} %param.49) | copy-start | bytes 393220
  276.8 13.2 %copy-start.9 = (f32[512]{0:T(512)S(1)}, f32[512]{0:T(512)}, u32[]{:S(2)}) copy-start(f32[512]{0:T(512)} %param.45) | copy-start | bytes 6148
where the time goes:
time: 317 us; the launch traced here: 315 us
  local copies, waits for them, and re-layouts  90.7 us (29%)
  waiting for transfers between devices  68 us (21%)
  matrix products  57 us (18%)
  starting transfers between devices  48.8 us (15%)
  blocking collectives  33 us (10%)
  other arithmetic  9.98 us (3%)
  between operations  7.49 us (2%)
    gather x1, local copies, waits for them, and re-layouts, body(): quarter[partition_edge_tail[0]]  57.8 us
    ppermute x8, waiting for transfers between devices, swapped(): return lax.ppermute(block, axis, route)  44.8 us
    dot_general x12, matrix products, accumulate(): jnp.einsum('mr,mw->rw', selector, part_values, preferred_element_type=jnp...  31.7 us
    ppermute x8, starting transfers between devices, swapped(): return lax.ppermute(block, axis, route)  26 us
    gather x1, local copies, waits for them, and re-layouts, body(): quarter[boundary_sender_vertex[0]]  24 us
    all_to_all x1, waiting for transfers between devices, body(): lax.all_to_all(outgoing, 'dom', split_axis=0, concat_axis=0, tiled=True)  23.2 us
    all_to_all x2, blocking collectives, sum_at_owner(): tiles = lax.all_to_all(cut_along(value, dim, size), axis, 0, 0, tiled=True)  21.7 us
    all_to_all x1, starting transfers between devices, body(): lax.all_to_all(live_slots.astype(jnp.bfloat16), 'dom', split_axis=0, conc...  13.2 us
  transfers between devices with their start and end apart: 10, of which 9 were waited for; matrix products, arithmetic and copies ran while one was open for 43% of the time, Pallas kernels for 0%

commit v1 on v0

v1 whole, which is shorter than its diff:
```python
import jax
import jax.numpy as jnp
from jax import lax
from jax.experimental import pallas as pl
from jax.experimental.pallas import tpu as pltpu
from jax.sharding import PartitionSpec as P

MESH = pl.DeviceIdType.MESH
BF16, F32, I32 = jnp.bfloat16, jnp.float32, jnp.int32
NY, NZ, NX = 4, 8, 4
ROWS = 512
LANES = 128
CAP = 128
SPLIT = 320
WROWS = 1280
EPSILON = 1e-05
LOG2E = 1.4426950408889634
MESSAGES = 220


class Net:
    def __init__(self, send_sems, recv_sems):
        self.send_sems, self.recv_sems = send_sems, recv_sems
        self.count = 0
        self.open = []
        dom = lax.axis_index("dom")
        self.m = lax.axis_index("mp")
        y, z = lax.div(dom, 2 * NZ), lax.rem(lax.div(dom, 2), NZ)
        self.c = lax.rem(dom, 2)
        self.me = dom
        self.ys = [lax.rem(y + k, NY) for k in range(NY)]
        self.zs = [lax.rem(z + k, NZ) for k in range(NZ)]
        self.ms = [lax.rem(self.m + k, NX) for k in range(NX)]

    def dom(self, dy, dz, other=0):
        core = 1 - self.c if other else self.c
        return (self.ys[dy % NY] * NZ + self.zs[dz % NZ]) * 2 + core

    def at(self, dy, dz, other=0):
        return {"dom": self.dom(dy, dz, other)}

    def along(self, k):
        return {"mp": self.ms[k % NX]}

    def send(self, src, dst, device, landing):
        i = self.count
        self.count += 1
        copy = pltpu.make_async_remote_copy(
            src_ref=src, dst_ref=dst, send_sem=self.send_sems.at[i], recv_sem=self.recv_sems.at[i],
            device_id=device, device_id_type=MESH)
        copy.start()
        self.open.append(copy)
        arrival = pltpu.make_async_remote_copy(
            src_ref=landing, dst_ref=landing, send_sem=self.send_sems.at[i], recv_sem=self.recv_sems.at[i],
            device_id=device, device_id_type=MESH)
        return arrival.wait_recv

    def finish(self):
        for copy in self.open:
            copy.wait_send()


def half(low, high, sign):
    middle = (low + high) // 2
    return (low, middle) if sign > 0 else (middle, high)


class TorusGather:
    def __init__(self, net, blocks):
        self.net, self.blocks = net, blocks
        self.pending = [[] for _ in range(9)]
        self.twins = [[] for _ in range(9)]
        self.got = {}

    def piece(self, block, low, high):
        return self.blocks.at[block, pl.ds(low, high - low), :]

    def have(self, dy, dz, low, high, level):
        key = (dy % NY, dz % NZ)
        self.got[key] = self.got.get(key, 0) + high - low
        if self.got[key] == ROWS:
            net = self.net
            src = self.blocks.at[net.dom(*key)]
            wait = net.send(src, src, net.at(0, 0, 1), self.blocks.at[net.dom(*key, 1)])
            self.twins[level + 1].append(wait)

    def hop(self, axis, sign, step, dy, dz, low, high, level, then):
        net = self.net
        ring = NY if axis == "y" else NZ
        hy, hz = (sign, 0) if axis == "y" else (0, sign)
        if step == ring // 2:
            low, high = half(low, high, sign)
        oy, oz = dy - hy, dz - hz
        src = self.piece(net.dom(dy, dz), low, high)
        wait = net.send(src, src, net.at(hy, hz), self.piece(net.dom(oy, oz), low, high))

        def arrived(now):
            wait()
            if step < ring // 2:
                self.hop(axis, sign, step + 1, oy, oz, low, high, now, then)
            if then is not None:
                for s in (1, -1):
                    self.hop(then, s, 1, oy, oz, low, high, now, None)
            self.have(oy, oz, low, high, now)

        self.pending[level + 1].append(arrived)

    def start(self):
        for s in (1, -1):
            self.hop("y", s, 1, 0, 0, SPLIT, ROWS, 0, "z")
            self.hop("z", s, 1, 0, 0, 0, SPLIT, 0, "y")
        for s in (1, -1):
            self.hop("z", s, 1, 0, 0, SPLIT, ROWS, 0, None)
            self.hop("y", s, 1, 0, 0, 0, SPLIT, 0, None)
        self.have(0, 0, 0, ROWS, 0)

    def events(self, level):
        return [lambda a=a: a(level) for a in self.pending[level]] + self.twins[level]


def normalize(parts, gains):
    parts = [p.astype(F32) for p in parts]
    width = sum(p.shape[1] for p in parts)
    mean = sum(jnp.sum(p, -1, keepdims=True) for p in parts) / width
    parts = [p - mean for p in parts]
    variance = sum(jnp.sum(p * p, -1, keepdims=True) for p in parts) / width
    scale = lax.rsqrt(variance + EPSILON)
    return [(p * scale * g).astype(BF16) for p, g in zip(parts, gains)]


def dot(a, b):
    return jnp.dot(a, b, preferred_element_type=F32)


def dot_nt(a, b):
    return lax.dot_general(a, b, (((1,), (1,)), ((), ())), preferred_element_type=F32)


def erf(x):
    x = jnp.clip(x, -3.832506856900711, 3.832506856900711)
    s = x * x
    top = jnp.full_like(s, 0.00022905065861350646)
    for k in (0.0034082910107109506, 0.050955695062380861, 0.18520832239976145, 1.128379143519084):
        top = top * s + k
    low = jnp.full_like(s, -1.1791602954361697e-7)
    for k in (0.000023547966471313185, 0.0010179625278914885, 0.014070470171167667, 0.11098505178285362,
              0.49746925110067538, 1.0):
        low = low * s + k
    return x * top / low


def one_hot(match):
    return jnp.where(match, 1.0, 0.0).astype(BF16)


def kernel(x_ref, gain1, gain2, wqkv, logit_scale, wf, wn, we, wc, match_ref, sender_ref, landing_ref,
           tail_ref, sink_ref, out_ref,
           blocks, wall, i1, i2, i3, spread, counts_f, counts, counts_in, q_s, k_s, v_s, m_s, l_s, o_s,
           att_s, att_in, bnd_s, bnd_in, picked, xp, send_sems, recv_sems, local_sems):
    net = Net(send_sems, recv_sems)
    m, c = net.m, net.c

    loads = []
    for k, (ref, low, high) in enumerate(((we, 0, 512), (wc, 512, 1024), (wf, 1024, 1152), (wn, 1152, 1280))):
        loads.append(pltpu.make_async_copy(ref, wall.at[m, pl.ds(low, high - low), :], local_sems.at[k]))
        loads[-1].start()

    blocks[net.me] = x_ref[:, pl.ds(pl.multiple_of(m * LANES, LANES), LANES)]
    barrier = pltpu.get_barrier_semaphore()
    peers = ([net.at(0, k) for k in range(1, NZ)] + [net.at(k, 0) for k in range(1, NY)]
             + [net.at(0, 0, 1)] + [net.along(k) for k in range(1, NX)])
    for peer in peers:
        pl.semaphore_signal(barrier, inc=1, device_id=peer, device_id_type=MESH)
    pl.semaphore_wait(barrier, len(peers))

    waits_z = []
    for k in range(1, NZ):
        waits_z.append(net.send(sender_ref.at[:, net.zs[k]], i1.at[NZ - k], net.at(0, k), i1.at[NZ - k]))
    i1[0] = sender_ref[:, net.zs[0]]

    gather = TorusGather(net, blocks)
    gather.start()

    for load in loads:
        load.wait()

    own_low = pl.multiple_of(c * (WROWS // 2), WROWS // 2)

    def rows(low, high):
        return pl.ds(own_low + low, high - low)

    ring_waits = []
    for s in (1, -1):
        src = wall.at[m, rows(0, 640), :]
        ring_waits.append(net.send(src, src, net.along(s), wall.at[net.ms[-s % NX], rows(0, 640), :]))

    gains = gain1[...]

    @pl.loop(0, 4)
    def _(r):
        sl = pl.ds(pl.multiple_of(r * 128, 128), 128)
        normed = normalize([x_ref[sl, :]], [gains])[0]
        q_s[sl, :] = dot(normed, wqkv[0]).astype(BF16)
        k_s[0, sl, :] = dot(normed, wqkv[1]).astype(BF16)
        v_s[0, sl, :] = dot(normed, wqkv[2]).astype(BF16)

    for wait in waits_z:
        wait()
    waits_y = []
    for k in range(1, NY):
        waits_y.append(net.send(i1.at[:, net.ys[k]], i2.at[NY - k], net.at(k, 0), i2.at[NY - k]))
    i2[0] = i1[:, net.ys[0]]

    def count_step(r):
        base = m * 32 + r * 4
        sub = lax.broadcasted_iota(I32, (ROWS, LANES), 0)
        sinks = jnp.concatenate([one_hot(sub == sink_ref[pl.ds(base + k, 1), :]) for k in range(4)], axis=1)
        tails = jnp.concatenate([one_hot(sub == tail_ref[pl.ds(base + k, 1), :]) for k in range(4)], axis=1)
        return dot_nt(sinks, tails)

    def count_chunk(low, high):
        @pl.loop(low, high)
        def _(r):
            counts_f[...] += count_step(r)

    def attend(j):
        lane = lax.broadcasted_iota(I32, (128, LANES), 1)

        @pl.loop(0, 4)
        def _(r):
            sl = pl.ds(pl.multiple_of(r * 128, 128), 128)
            q = q_s[sl, :]
            for h in range(2):
                mine = (lane >= 64) if h else (lane < 64)
                scores = dot_nt(jnp.where(mine, q, jnp.zeros_like(q)), k_s[j]) * (logit_scale[0, h] * LOG2E)
                top = jnp.max(scores, -1, keepdims=True)
                if j == 0:
                    p = jnp.exp2(scores - top)
                    l_s[h, sl, :] = jnp.broadcast_to(jnp.sum(p, -1, keepdims=True), (128, LANES))
                    o_s[h, sl, :] = dot(p.astype(BF16), v_s[j])
                    m_s[h, sl, :] = jnp.broadcast_to(top, (128, LANES))
                else:
                    old = m_s[h, sl, :]
                    new = jnp.maximum(old, top)
                    shrink = jnp.exp2(old - new)
                    p = jnp.exp2(scores - new[:, :1])
                    l_s[h, sl, :] = l_s[h, sl, :] * shrink + jnp.sum(p, -1, keepdims=True)
                    o_s[h, sl, :] = o_s[h, sl, :] * shrink + dot(p.astype(BF16), v_s[j])
                    m_s[h, sl, :] = new

    def spread_lists():
        for t in range(2):
            table = i3[t].reshape(NY * NZ, LANES).T
            for r in range(NY * NZ):
                spread[t, r // NZ, r % NZ] = jnp.broadcast_to(table[:, r:r + 1], (CAP, LANES))

    def land(dz, t):
        lane = lax.broadcasted_iota(I32, (CAP, ROWS), 1)
        sub = lax.broadcasted_iota(I32, (ROWS, LANES), 0)
        zz = lax.rem(net.zs[0] + dz, NZ)
        core = net.c + t - 2 * net.c * t
        targets = []
        for dy in range(NY):
            block = (net.ys[dy] * NZ + zz) * 2 + core
            index = spread[t, dy, dz]
            pick = one_hot(jnp.concatenate([index] * 4, axis=1) == lane)
            picked[pl.ds(dy * CAP, CAP), pl.ds(0, LANES)] = dot(pick, blocks[block]).astype(BF16)
            target = jnp.where(i3[t, dy, dz] >= 0, landing_ref[block], -1)
            targets.append(one_hot(sub == target))
        bnd_s[...] += dot(jnp.concatenate(targets, axis=1), picked[...])

    def land_level(level):
        if 2 <= level <= 6:
            land_pair(level - 2, 0)
        if 3 <= level <= 7:
            land_pair(level - 3, 1)

    def land_pair(dz, t):
        if dz in (0, 4):
            land(dz, t)
        else:
            @pl.loop(0, 2)
            def _(k):
                land(dz + k * (NZ - 2 * dz), t)

    counts_f[...] = jnp.zeros_like(counts_f)
    bnd_s[...] = jnp.zeros_like(bnd_s)
    picked[:, pl.ds(LANES, LANES)] = jnp.ones((ROWS, LANES), BF16)
    count_chunk(0, 2)
    for event in gather.events(1):
        event()
    for wait in waits_y:
        wait()
    other = pl.multiple_of((1 - c) * LANES, LANES)
    wait_twin = net.send(i2.at[:, :, :, pl.ds(other, LANES)], i3.at[1], net.at(0, 0, 1), i3.at[1])
    i3[0] = i2[:, :, :, pl.ds(pl.multiple_of(c * LANES, LANES), LANES)]
    count_chunk(2, 5)
    wait_twin()
    for event in gather.events(2):
        event()
    count_chunk(5, 8)
    counts[...] = counts_f[...].astype(jnp.int16)
    count_waits = []
    for k in range(1, NX):
        count_waits.append(net.send(
            counts.at[pl.ds(pl.multiple_of(net.ms[k] * 128, 128), 128), :], counts_in.at[NX - k],
            net.along(k), counts_in.at[NX - k]))
    counts_in[0] = counts[pl.ds(pl.multiple_of(m * 128, 128), 128), :]
    spread_lists()
    land_level(2)
    for event in gather.events(3):
        event()
    land_level(3)
    attend(0)
    for wait in ring_waits:
        wait()
    ring_second = []
    for s in (1, -1):
        low, high = half(0, 640, s)
        src = wall.at[net.ms[-s % NX], rows(low, high), :]
        ring_second.append(net.send(src, src, net.along(s), wall.at[net.ms[2], rows(low, high), :]))
    twin_low = pl.multiple_of((1 - c) * (WROWS // 2), WROWS // 2)
    twin_waits = []

    def to_twin(k):
        src = wall.at[net.ms[k], rows(0, 640), :]
        twin_waits.append(net.send(src, src, net.at(0, 0, 1), wall.at[net.ms[k], pl.ds(twin_low, 640), :]))

    to_twin(1)
    to_twin(3)
    for level in (4, 5):
        for event in gather.events(level):
            event()
        land_level(level)
    for level in (6, 7):
        for event in gather.events(level):
            event()

    pair_waits = []
    for j in range(2):
        xp[j, m] = blocks[match_ref[j, net.me]]
        src = xp.at[j, m]
        pair_waits.append([net.send(src, src, net.along(k), xp.at[j, net.ms[NX - k]]) for k in range(1, NX)])
    for wait in ring_second:
        wait()
    to_twin(2)
    land_level(6)
    land_level(7)

    final_waits = []
    for k in range(1, NX):
        final_waits.append(net.send(
            bnd_s.at[pl.ds(pl.multiple_of(net.ms[k] * 128, 128), 128), pl.ds(0, LANES)], bnd_in.at[m],
            net.along(k), bnd_in.at[net.ms[NX - k]]))
    own_rows = pl.ds(pl.multiple_of(m * 128, 128), 128)
    bnd_in[m] = bnd_s[own_rows, pl.ds(0, LANES)]

    for wait in count_waits:
        wait()
    total = (counts_in[0].astype(F32) + counts_in[1].astype(F32)
             + counts_in[2].astype(F32) + counts_in[3].astype(F32))
    coarse = total.astype(BF16)
    fine = (total - coarse.astype(F32)).astype(BF16)
    local_sum = dot(coarse, x_ref[...]) + dot(fine, x_ref[...])
    degree = bnd_s[own_rows, pl.ds(LANES, 1)] + jnp.sum(total, -1, keepdims=True)
    x_own = x_ref[own_rows, :].astype(F32)
    base = x_own + local_sum

    for j in range(2):
        for wait in pair_waits[j]:
            wait()

        @pl.loop(0, 4)
        def _(r):
            sl = pl.ds(pl.multiple_of(r * 128, 128), 128)
            normed = normalize([xp[j, k, sl, :] for k in range(NX)],
                               [gain1[:, pl.ds(k * LANES, LANES)] for k in range(NX)])
            normed = jnp.concatenate(normed, axis=1)
            k_s[j + 1, sl, :] = dot(normed, wqkv[1]).astype(BF16)
            v_s[j + 1, sl, :] = dot(normed, wqkv[2]).astype(BF16)

        attend(j + 1)

    lane = lax.broadcasted_iota(I32, (ROWS, LANES), 1)
    att_s[...] = jnp.where(lane < 64, o_s[0] / l_s[0], o_s[1] / l_s[1]).astype(BF16)
    att_waits = []
    for k in range(1, NX):
        att_waits.append(net.send(
            att_s.at[pl.ds(pl.multiple_of(net.ms[k] * 128, 128), 128), :], att_in.at[m],
            net.along(k), att_in.at[net.ms[NX - k]]))
    att_in[m] = att_s[own_rows, :]

    for wait in twin_waits + final_waits:
        wait()
    message = (base + jnp.concatenate([bnd_in[k] for k in range(NX)], axis=1)) / (1.0 + degree)
    message = message.astype(BF16)
    mixed = x_own
    for k in range(NX):
        mixed += dot(message[:, k * 128:(k + 1) * 128], wall[k, pl.ds(1152, 128), :])
    for wait in att_waits:
        wait()
    for k in range(NX):
        mixed += dot(att_in[k], wall[k, pl.ds(1024, 128), :])
    normed = normalize([mixed], [gain2[...]])[0]
    total_s = counts_f.at[pl.ds(0, 128), :]
    total_s[...] = mixed

    @pl.loop(0, NX)
    def _(k):
        hidden = dot(normed, wall[k, pl.ds(0, 512), :])
        hidden = (hidden * 0.5 * (1.0 + erf(hidden * 0.7071067811865476))).astype(BF16)
        total_s[...] += dot(hidden, wall[k, pl.ds(512, 512), :])

    out_ref[...] = total_s[...].astype(BF16)
    net.finish()


def body(vertex_embedding, prenorm_mixer_scale, prenorm_perceptron_scale, triple_projector_stack,
         channel_logit_scaling, mixer_final_projector, neighbour_mixer_projector, expand_projector,
         contract_projector, matched_companion, boundary_sender_vertex, boundary_slot_tally,
         boundary_landing_vertex, partition_edge_tail, partition_edge_sink):
    slot = jnp.arange(CAP, dtype=I32)
    sender = jnp.where(slot[None, :] < boundary_slot_tally[0][:, None], boundary_sender_vertex[0], -1)
    vmem = pl.BlockSpec(memory_space=pltpu.VMEM)
    smem = pl.BlockSpec(memory_space=pltpu.SMEM)
    anywhere = pl.BlockSpec(memory_space=pl.ANY)
    return pl.pallas_call(
        kernel,
        name="layer",
        out_shape=jax.ShapeDtypeStruct((128, 512), BF16),
        in_specs=[vmem, vmem, vmem, vmem, smem, anywhere, anywhere, anywhere, anywhere, smem, vmem, vmem, vmem, vmem],
        out_specs=vmem,
        scratch_shapes=[
            pltpu.VMEM((64, ROWS, LANES), BF16),
            pltpu.VMEM((NX, WROWS, 512), BF16),
            pltpu.VMEM((NZ, NY, 1, 2 * CAP), I32),
            pltpu.VMEM((NY, NZ, 1, 2 * CAP), I32),
            pltpu.VMEM((2, NY, NZ, 1, CAP), I32),
            pltpu.VMEM((2, NY, NZ, CAP, LANES), I32),
            pltpu.VMEM((ROWS, ROWS), F32),
            pltpu.VMEM((ROWS, ROWS), jnp.int16),
            pltpu.VMEM((NX, 128, ROWS), jnp.int16),
            pltpu.VMEM((ROWS, LANES), BF16),
            pltpu.VMEM((3, ROWS, LANES), BF16),
            pltpu.VMEM((3, ROWS, LANES), BF16),
            pltpu.VMEM((2, ROWS, LANES), F32),
            pltpu.VMEM((2, ROWS, LANES), F32),
            pltpu.VMEM((2, ROWS, LANES), F32),
            pltpu.VMEM((ROWS, LANES), BF16),
            pltpu.VMEM((NX, 128, LANES), BF16),
            pltpu.VMEM((ROWS, 2 * LANES), F32),
            pltpu.VMEM((NX, 128, LANES), F32),
            pltpu.VMEM((ROWS, 2 * LANES), BF16),
            pltpu.VMEM((2, NX, ROWS, LANES), BF16),
            pltpu.SemaphoreType.DMA((MESSAGES,)),
            pltpu.SemaphoreType.DMA((MESSAGES,)),
            pltpu.SemaphoreType.DMA((4,)),
        ],
        compiler_params=pltpu.CompilerParams(
            collective_id=0, has_side_effects=True, vmem_limit_bytes=56 << 20),
    )(
        vertex_embedding,
        prenorm_mixer_scale.reshape(1, 512),
        prenorm_perceptron_scale.reshape(1, 512),
        triple_projector_stack,
        channel_logit_scaling.reshape(1, 2),
        mixer_final_projector,
        neighbour_mixer_projector,
        expand_projector,
        contract_projector,
        matched_companion,
        sender.reshape(NY, NZ, 1, 2 * CAP),
        boundary_landing_vertex.reshape(64, 1, CAP),
        partition_edge_tail.reshape(128, LANES),
        partition_edge_sink.reshape(128, LANES),
    )


def solution(mesh):
    return jax.shard_map(
        body,
        mesh=mesh,
        in_specs=(
            P("dom", None),
            P(),
            P(),
            P(None, None, "mp"),
            P("mp"),
            P("mp", None),
            P("mp", None),
            P(None, "mp"),
            P("mp", None),
            P(),
            P("dom", None, None),
            P("dom", None),
            P("dom", None, None),
            P("dom", None),
            P("dom", None),
        ),
        out_specs=P(("dom", "mp"), None),
        check_vma=False,
    )
```

time: 317 us -> 78.8 us (0.25)
  local copies, waits for them, and re-layouts: 90.7 us -> 2.96 us
  Pallas kernels: 0 us -> 74.2 us
  waiting for transfers between devices: 68 us -> 0 us
  matrix products: 57 us -> 0 us
  starting transfers between devices: 48.8 us -> 0 us
  blocking collectives: 33 us -> 0 us
  other arithmetic: 9.98 us -> 1.32 us
  between operations: 7.49 us -> 0.04 us
    gather x2 -> x0, local copies, waits for them, and re-layouts: 81.8 us -> none  [the longest x1 57.8 us: body(): quarter[partition_edge_tail[0]]]
    pallas_call x0 -> x1, Pallas kernels: none -> 74.2 us  [body(): pl.pallas_call(kernel, name='layer', out_shape=jax.ShapeDtypeStruct((128,...]
    dot_general x28 -> x0, matrix products: 49.8 us -> none  [the longest x12 31.7 us: accumulate(): jnp.einsum('mr,mw->rw', selector, part_values, preferred_element_type=jnp...]
    ppermute x8 -> x0, waiting for transfers between devices: 44.8 us -> none  [swapped(): return lax.ppermute(block, axis, route)]
    ppermute x8 -> x0, starting transfers between devices: 26 us -> none  [swapped(): return lax.ppermute(block, axis, route)]
    all_to_all x2 -> x0, waiting for transfers between devices: 23.2 us -> none  [the longest x1 23.2 us: body(): lax.all_to_all(outgoing, 'dom', split_axis=0, concat_axis=0, tiled=True)]
    all_to_all x2 -> x0, starting transfers between devices: 22.8 us -> none  [the longest x1 13.2 us: body(): lax.all_to_all(live_slots.astype(jnp.bfloat16), 'dom', split_axis=0, conc...]
    all_to_all x2 -> x0, blocking collectives: 21.7 us -> none  [sum_at_owner(): tiles = lax.all_to_all(cut_along(value, dim, size), axis, 0, 0, tiled=True)]
  transfers between devices with their start and end apart: 10 -> 0, of which waited for: 9 -> 0; matrix products, arithmetic and copies ran while one was open for 43% -> 0% of each run, Pallas kernels for 0% -> 0%
where the time goes in v1:
time: 78.8 us; the launch traced here: 78.6 us
  Pallas kernels  74.2 us (94%)
  local copies, waits for them, and re-layouts  2.96 us (4%)
  other arithmetic  1.32 us (2%)
    pallas_call x1, Pallas kernels, body(): pl.pallas_call(kernel, name='layer', out_shape=jax.ShapeDtypeStruct((128,...  74.2 us
    unnamed x6, local copies, waits for them, and re-layouts  2.77 us

profile of v1, /device:TPU:1, one launch (start us, length us, event | category | flops | bytes accessed | tf_op | source)
XLA Modules:
  0.0 78.6 jit_solution(14373337334196242531)
XLA Ops:
  0.0 0.0 copy-start.1
  0.0 0.5 broadcast.22
  0.5 0.1 copy-done.1
  0.7 0.7 reduce.3
  1.3 0.0 copy-start
  1.3 0.1 lt.31
  1.4 0.1 lt.32
  1.5 0.5 copy-done
  2.1 0.7 compare_select_fusion.sender_ref
  2.8 74.2 %layer.1 = bf16[128,512]{1,0:T(8,128)(2,1)} custom-call(bf16[512,512]{1,0:T(8,128)(2,1)} %x_ref.1, f32[1,512]{1,0:T(1,128)} %bitcast.15, f32[1,512]{1,0:T(1,128)} %bitcast.16, bf16[3,512,128]{2,1,0:T(8,128)(2,1)} %wqkv.1, f32[1,2]{1,0:T(1,128)} %bitcast.17, bf16[128,512]{1,0:T(8,128)(2,1)} %wf.1, bf16[128,512]{1,0:T(8,128)(2,1)} %wn.1, bf16[512,512]{1,0:T(8,128)(2,1)} %we.1, ...), custom_call_target="tpu_custom_call" | custom-call | tf_op jit(solution)/shard_map/layer/pallas_call | solution.py:427
  77.0 1.6 %copy.17 = bf16[128,512]{1,0:T(8,128)(2,1)} copy(bf16[128,512]{1,0:T(8,128)(2,1)} %layer.1) | data formatting | bytes 262144
  (1 shorter events, 0.0 us)
Async XLA Ops:
  0.0 0.7 copy-start.1
  1.3 0.8 copy-start

commit v2 on v1

--- a/solution.py
+++ b/solution.py
@@ -153,30 +153,40 @@
     return jnp.where(match, 1.0, 0.0).astype(BF16)
 
 
-def kernel(x_ref, gain1, gain2, wqkv, logit_scale, wf, wn, we, wc, match_ref, sender_ref, landing_ref,
+def kernel(x_ref, gain1, gain2, wqkv, logit_scale, wf, wn, we, wc, match_ref, sender_ref, tally_ref, landing_ref,
            tail_ref, sink_ref, out_ref,
-           blocks, wall, i1, i2, i3, spread, counts_f, counts, counts_in, q_s, k_s, v_s, m_s, l_s, o_s,
+           blocks, wall, i0, i1, i2, i3, spread, counts_f, counts, counts_in, q_s, k_s, v_s, m_s, o_s,
            att_s, att_in, bnd_s, bnd_in, picked, xp, send_sems, recv_sems, local_sems):
     net = Net(send_sems, recv_sems)
     m, c = net.m, net.c
+
+    def rows128(k):
+        return pl.ds(pl.multiple_of(k * 128, 128), 128)
+
+    own_rows = rows128(m)
 
     loads = []
     for k, (ref, low, high) in enumerate(((we, 0, 512), (wc, 512, 1024), (wf, 1024, 1152), (wn, 1152, 1280))):
         loads.append(pltpu.make_async_copy(ref, wall.at[m, pl.ds(low, high - low), :], local_sems.at[k]))
         loads[-1].start()
 
-    blocks[net.me] = x_ref[:, pl.ds(pl.multiple_of(m * LANES, LANES), LANES)]
+    blocks[net.me] = x_ref[:, rows128(m)]
     barrier = pltpu.get_barrier_semaphore()
     peers = ([net.at(0, k) for k in range(1, NZ)] + [net.at(k, 0) for k in range(1, NY)]
              + [net.at(0, 0, 1)] + [net.along(k) for k in range(1, NX)])
     for peer in peers:
         pl.semaphore_signal(barrier, inc=1, device_id=peer, device_id_type=MESH)
+
+    lane_row = lax.broadcasted_iota(I32, (1, CAP), 1)
+    for d in range(64):
+        live = jnp.where(lane_row < tally_ref[0, d], sender_ref[d], -1)
+        i0[d // 16, (d // 2) % 8, :, pl.ds((d % 2) * CAP, CAP)] = live
     pl.semaphore_wait(barrier, len(peers))
 
     waits_z = []
     for k in range(1, NZ):
-        waits_z.append(net.send(sender_ref.at[:, net.zs[k]], i1.at[NZ - k], net.at(0, k), i1.at[NZ - k]))
-    i1[0] = sender_ref[:, net.zs[0]]
+        waits_z.append(net.send(i0.at[:, net.zs[k]], i1.at[NZ - k], net.at(0, k), i1.at[NZ - k]))
+    i1[0] = i0[:, net.zs[0]]
 
     gather = TorusGather(net, blocks)
     gather.start()
@@ -194,65 +204,78 @@
         src = wall.at[m, rows(0, 640), :]
         ring_waits.append(net.send(src, src, net.along(s), wall.at[net.ms[-s % NX], rows(0, 640), :]))
 
-    gains = gain1[...]
-
-    @pl.loop(0, 4)
-    def _(r):
-        sl = pl.ds(pl.multiple_of(r * 128, 128), 128)
-        normed = normalize([x_ref[sl, :]], [gains])[0]
-        q_s[sl, :] = dot(normed, wqkv[0]).astype(BF16)
-        k_s[0, sl, :] = dot(normed, wqkv[1]).astype(BF16)
-        v_s[0, sl, :] = dot(normed, wqkv[2]).astype(BF16)
-
-    for wait in waits_z:
-        wait()
-    waits_y = []
-    for k in range(1, NY):
-        waits_y.append(net.send(i1.at[:, net.ys[k]], i2.at[NY - k], net.at(k, 0), i2.at[NY - k]))
-    i2[0] = i1[:, net.ys[0]]
-
-    def count_step(r):
-        base = m * 32 + r * 4
-        sub = lax.broadcasted_iota(I32, (ROWS, LANES), 0)
-        sinks = jnp.concatenate([one_hot(sub == sink_ref[pl.ds(base + k, 1), :]) for k in range(4)], axis=1)
-        tails = jnp.concatenate([one_hot(sub == tail_ref[pl.ds(base + k, 1), :]) for k in range(4)], axis=1)
-        return dot_nt(sinks, tails)
+    lane128 = lax.broadcasted_iota(I32, (128, LANES), 1)
+
+    def put_values(j, sl, values):
+        values = values.astype(BF16)
+        ones = jnp.ones_like(values)
+        v_s[0, j, sl, :] = jnp.where(lane128 < 64, values, ones)
+        v_s[1, j, sl, :] = jnp.where(lane128 < 64, ones, values)
+
+    def project(low, high):
+        @pl.loop(low, high)
+        def _(r):
+            sl = rows128(r)
+            normed = normalize([x_ref[sl, :]], [gain1[...]])[0]
+            q_s[sl, :] = dot(normed, wqkv[0]).astype(BF16)
+            k_s[0, sl, :] = dot(normed, wqkv[1]).astype(BF16)
+            put_values(0, sl, dot(normed, wqkv[2]))
+
+    def pair_project(j):
+        @pl.loop(0, 4)
+        def _(r):
+            sl = rows128(r)
+            normed = normalize([xp[j, k, sl, :] for k in range(NX)],
+                               [gain1[:, pl.ds(k * LANES, LANES)] for k in range(NX)])
+            normed = jnp.concatenate(normed, axis=1)
+            k_s[j + 1, sl, :] = dot(normed, wqkv[1]).astype(BF16)
+            put_values(j + 1, sl, dot(normed, wqkv[2]))
 
     def count_chunk(low, high):
         @pl.loop(low, high)
         def _(r):
-            counts_f[...] += count_step(r)
+            base = m * 32 + r * 4
+            sub = lax.broadcasted_iota(I32, (ROWS, LANES), 0)
+            sinks = jnp.concatenate([one_hot(sub == sink_ref[pl.ds(base + k, 1), :]) for k in range(4)], axis=1)
+            tails = jnp.concatenate([one_hot(sub == tail_ref[pl.ds(base + k, 1), :]) for k in range(4)], axis=1)
+            counts_f[...] += dot_nt(sinks, tails)
+
+    count_waits = []
+
+    def count_send():
+        counts[...] = counts_f[...].astype(jnp.int16)
+        for k in (2, 1, 3):
+            count_waits.append(net.send(
+                counts.at[rows128(net.ms[k]), :], counts_in.at[NX - k], net.along(k), counts_in.at[NX - k]))
+        counts_in[0] = counts[own_rows, :]
+
+    def attend_rows(j, sl):
+        q = q_s[sl, :]
+        for h in range(2):
+            mine = (lane128 >= 64) if h else (lane128 < 64)
+            scores = dot_nt(jnp.where(mine, q, jnp.zeros_like(q)), k_s[j]) * (logit_scale[0, h] * LOG2E)
+            top = jnp.max(scores, -1, keepdims=True)
+            if j == 0:
+                p = jnp.exp2(scores - top)
+                o_s[h, sl, :] = dot(p.astype(BF16), v_s[h, j])
+                m_s[h, sl, :] = jnp.broadcast_to(top, (128, LANES))
+            else:
+                old = m_s[h, sl, :]
+                new = jnp.maximum(old, top)
+                p = jnp.exp2(scores - new[:, :1])
+                o_s[h, sl, :] = o_s[h, sl, :] * jnp.exp2(old - new) + dot(p.astype(BF16), v_s[h, j])
+                m_s[h, sl, :] = new
 
     def attend(j):
-        lane = lax.broadcasted_iota(I32, (128, LANES), 1)
-
-        @pl.loop(0, 4)
-        def _(r):
-            sl = pl.ds(pl.multiple_of(r * 128, 128), 128)
-            q = q_s[sl, :]
-            for h in range(2):
-                mine = (lane >= 64) if h else (lane < 64)
-                scores = dot_nt(jnp.where(mine, q, jnp.zeros_like(q)), k_s[j]) * (logit_scale[0, h] * LOG2E)
-                top = jnp.max(scores, -1, keepdims=True)
-                if j == 0:
-                    p = jnp.exp2(scores - top)
-                    l_s[h, sl, :] = jnp.broadcast_to(jnp.sum(p, -1, keepdims=True), (128, LANES))
-                    o_s[h, sl, :] = dot(p.astype(BF16), v_s[j])
-                    m_s[h, sl, :] = jnp.broadcast_to(top, (128, LANES))
-                else:
-                    old = m_s[h, sl, :]
-                    new = jnp.maximum(old, top)
-                    shrink = jnp.exp2(old - new)
-                    p = jnp.exp2(scores - new[:, :1])
-                    l_s[h, sl, :] = l_s[h, sl, :] * shrink + jnp.sum(p, -1, keepdims=True)
-                    o_s[h, sl, :] = o_s[h, sl, :] * shrink + dot(p.astype(BF16), v_s[j])
-                    m_s[h, sl, :] = new
-
-    def spread_lists():
-        for t in range(2):
-            table = i3[t].reshape(NY * NZ, LANES).T
-            for r in range(NY * NZ):
-                spread[t, r // NZ, r % NZ] = jnp.broadcast_to(table[:, r:r + 1], (CAP, LANES))
+        @pl.loop(0, 2)
+        def _(half):
+            for r in range(2):
+                attend_rows(j, rows128(half * 2 + r))
+
+    def spread_lists(t):
+        table = i3[t].reshape(NY * NZ, LANES).T
+        for r in range(NY * NZ):
+            spread[t, r // NZ, r % NZ] = jnp.broadcast_to(table[:, r:r + 1], (CAP, LANES))
 
     def land(dz, t):
         lane = lax.broadcasted_iota(I32, (CAP, ROWS), 1)
@@ -269,12 +292,6 @@
             targets.append(one_hot(sub == target))
         bnd_s[...] += dot(jnp.concatenate(targets, axis=1), picked[...])
 
-    def land_level(level):
-        if 2 <= level <= 6:
-            land_pair(level - 2, 0)
-        if 3 <= level <= 7:
-            land_pair(level - 3, 1)
-
     def land_pair(dz, t):
         if dz in (0, 4):
             land(dz, t)
@@ -283,77 +300,92 @@
             def _(k):
                 land(dz + k * (NZ - 2 * dz), t)
 
+    waits_y, wait_c = [], []
+
+    def lists_y():
+        for wait in waits_z:
+            wait()
+        for k in range(1, NY):
+            waits_y.append(net.send(i1.at[:, net.ys[k]], i2.at[NY - k], net.at(k, 0), i2.at[NY - k]))
+        i2[0] = i1[:, net.ys[0]]
+
+    def lists_c():
+        for wait in waits_y:
+            wait()
+        other = pl.multiple_of((1 - c) * CAP, CAP)
+        wait_c.append(net.send(i2.at[:, :, :, pl.ds(other, CAP)], i3.at[1], net.at(0, 0, 1), i3.at[1]))
+        i3[0] = i2[:, :, :, pl.ds(pl.multiple_of(c * CAP, CAP), CAP)]
+
+    def lists_end():
+        wait_c[0]()
+
+    ring_second, twin_waits = [], []
+    twin_low = pl.multiple_of((1 - c) * (WROWS // 2), WROWS // 2)
+
+    def to_twin(k):
+        src = wall.at[net.ms[k], rows(0, 640), :]
+        twin_waits.append(net.send(src, src, net.at(0, 0, 1), wall.at[net.ms[k], pl.ds(twin_low, 640), :]))
+
+    def weights_second():
+        for wait in ring_waits:
+            wait()
+        for s in (1, -1):
+            low, high = half(0, 640, s)
+            src = wall.at[net.ms[-s % NX], rows(low, high), :]
+            ring_second.append(net.send(src, src, net.along(s), wall.at[net.ms[2], rows(low, high), :]))
+        to_twin(1)
+        to_twin(3)
+
+    def level(number, tasks=()):
+        events = gather.events(number)
+        for i, event in enumerate(events):
+            event()
+            for task in tasks[i * len(tasks) // len(events):(i + 1) * len(tasks) // len(events)]:
+                task()
+
+    def run(fn, *args):
+        return lambda: fn(*args)
+
     counts_f[...] = jnp.zeros_like(counts_f)
     bnd_s[...] = jnp.zeros_like(bnd_s)
     picked[:, pl.ds(LANES, LANES)] = jnp.ones((ROWS, LANES), BF16)
-    count_chunk(0, 2)
-    for event in gather.events(1):
-        event()
-    for wait in waits_y:
-        wait()
-    other = pl.multiple_of((1 - c) * LANES, LANES)
-    wait_twin = net.send(i2.at[:, :, :, pl.ds(other, LANES)], i3.at[1], net.at(0, 0, 1), i3.at[1])
-    i3[0] = i2[:, :, :, pl.ds(pl.multiple_of(c * LANES, LANES), LANES)]
-    count_chunk(2, 5)
-    wait_twin()
-    for event in gather.events(2):
-        event()
-    count_chunk(5, 8)
-    counts[...] = counts_f[...].astype(jnp.int16)
-    count_waits = []
-    for k in range(1, NX):
-        count_waits.append(net.send(
-            counts.at[pl.ds(pl.multiple_of(net.ms[k] * 128, 128), 128), :], counts_in.at[NX - k],
-            net.along(k), counts_in.at[NX - k]))
-    counts_in[0] = counts[pl.ds(pl.multiple_of(m * 128, 128), 128), :]
-    spread_lists()
-    land_level(2)
-    for event in gather.events(3):
-        event()
-    land_level(3)
-    attend(0)
-    for wait in ring_waits:
-        wait()
-    ring_second = []
-    for s in (1, -1):
-        low, high = half(0, 640, s)
-        src = wall.at[net.ms[-s % NX], rows(low, high), :]
-        ring_second.append(net.send(src, src, net.along(s), wall.at[net.ms[2], rows(low, high), :]))
-    twin_low = pl.multiple_of((1 - c) * (WROWS // 2), WROWS // 2)
-    twin_waits = []
-
-    def to_twin(k):
-        src = wall.at[net.ms[k], rows(0, 640), :]
-        twin_waits.append(net.send(src, src, net.at(0, 0, 1), wall.at[net.ms[k], pl.ds(twin_low, 640), :]))
-
-    to_twin(1)
-    to_twin(3)
-    for level in (4, 5):
-        for event in gather.events(level):
-            event()
-        land_level(level)
-    for level in (6, 7):
-        for event in gather.events(level):
-            event()
-
-    pair_waits = []
+
+    project(0, 2)
+    level(1, [run(project, 2, 4)])
+    lists_y()
+    level(2, [run(count_chunk, k, k + 2) for k in range(0, 8, 2)] + [count_send])
+    lists_c()
+    level(3, [run(attend, 0), lists_end, run(spread_lists, 0), run(spread_lists, 1),
+              run(land_pair, 0, 0)])
+    level(4, [run(land_pair, 1, 0), weights_second, run(land_pair, 0, 1)])
+    level(5, [run(land_pair, 2, 0), run(land_pair, 1, 1)])
+    level(6)
+    level(7)
+
+    def exchange(j):
+        src = xp.at[j, m]
+        return [net.send(src, src, net.along(k), xp.at[j, net.ms[NX - k]]) for k in (2, 1, 3)]
+
     for j in range(2):
         xp[j, m] = blocks[match_ref[j, net.me]]
-        src = xp.at[j, m]
-        pair_waits.append([net.send(src, src, net.along(k), xp.at[j, net.ms[NX - k]]) for k in range(1, NX)])
+    first_pair = exchange(0)
+    for dz, t in ((3, 0), (2, 1), (4, 0), (3, 1), (4, 1)):
+        land_pair(dz, t)
     for wait in ring_second:
         wait()
     to_twin(2)
-    land_level(6)
-    land_level(7)
+    for wait in first_pair:
+        wait()
+    second_pair = exchange(1)
 
     final_waits = []
-    for k in range(1, NX):
-        final_waits.append(net.send(
-            bnd_s.at[pl.ds(pl.multiple_of(net.ms[k] * 128, 128), 128), pl.ds(0, LANES)], bnd_in.at[m],
-            net.along(k), bnd_in.at[net.ms[NX - k]]))
-    own_rows = pl.ds(pl.multiple_of(m * 128, 128), 128)
+    for k in (2, 1, 3):
+        final_waits.append(net.send(bnd_s.at[rows128(net.ms[k]), pl.ds(0, LANES)], bnd_in.at[m],
+                                    net.along(k), bnd_in.at[net.ms[NX - k]]))
     bnd_in[m] = bnd_s[own_rows, pl.ds(0, LANES)]
+
+    pair_project(0)
+    attend(1)
 
     for wait in count_waits:
         wait()
@@ -361,40 +393,33 @@
              + counts_in[2].astype(F32) + counts_in[3].astype(F32))
     coarse = total.astype(BF16)
     fine = (total - coarse.astype(F32)).astype(BF16)
-    local_sum = dot(coarse, x_ref[...]) + dot(fine, x_ref[...])
-    degree = bnd_s[own_rows, pl.ds(LANES, 1)] + jnp.sum(total, -1, keepdims=True)
-    x_own = x_ref[own_rows, :].astype(F32)
-    base = x_own + local_sum
-
-    for j in range(2):
-        for wait in pair_waits[j]:
-            wait()
-
-        @pl.loop(0, 4)
-        def _(r):
-            sl = pl.ds(pl.multiple_of(r * 128, 128), 128)
-            normed = normalize([xp[j, k, sl, :] for k in range(NX)],
-                               [gain1[:, pl.ds(k * LANES, LANES)] for k in range(NX)])
-            normed = jnp.concatenate(normed, axis=1)
-            k_s[j + 1, sl, :] = dot(normed, wqkv[1]).astype(BF16)
-            v_s[j + 1, sl, :] = dot(normed, wqkv[2]).astype(BF16)
-
-        attend(j + 1)
-
-    lane = lax.broadcasted_iota(I32, (ROWS, LANES), 1)
-    att_s[...] = jnp.where(lane < 64, o_s[0] / l_s[0], o_s[1] / l_s[1]).astype(BF16)
+    base_s = counts_f.at[own_rows, :]
+    degree = 1.0 + bnd_s[own_rows, pl.ds(LANES, 1)] + jnp.sum(total, -1, keepdims=True)
+    base_s[...] = x_ref[own_rows, :].astype(F32) + dot(coarse, x_ref[...]) + dot(fine, x_ref[...])
+
+    for wait in second_pair:
+        wait()
+    pair_project(1)
+
     att_waits = []
-    for k in range(1, NX):
-        att_waits.append(net.send(
-            att_s.at[pl.ds(pl.multiple_of(net.ms[k] * 128, 128), 128), :], att_in.at[m],
-            net.along(k), att_in.at[net.ms[NX - k]]))
-    att_in[m] = att_s[own_rows, :]
+    for k in (2, 1, 3, 0):
+        sl = rows128(net.ms[k])
+        attend_rows(2, sl)
+        first, second = o_s[0, sl, :], o_s[1, sl, :]
+        values = jnp.where(lane128 < 64, first, second)
+        sums = jnp.where(lane128 < 64, pltpu.roll(first, 64, 1), pltpu.roll(second, 64, 1))
+        attended = (values / sums).astype(BF16)
+        if k == 0:
+            att_in[m] = attended
+        else:
+            att_s[sl, :] = attended
+            att_waits.append(net.send(att_s.at[sl, :], att_in.at[m], net.along(k), att_in.at[net.ms[NX - k]]))
 
     for wait in twin_waits + final_waits:
         wait()
-    message = (base + jnp.concatenate([bnd_in[k] for k in range(NX)], axis=1)) / (1.0 + degree)
+    message = (base_s[...] + jnp.concatenate([bnd_in[k] for k in range(NX)], axis=1)) / degree
     message = message.astype(BF16)
-    mixed = x_own
+    mixed = x_ref[own_rows, :].astype(F32)
     for k in range(NX):
         mixed += dot(message[:, k * 128:(k + 1) * 128], wall[k, pl.ds(1152, 128), :])
     for wait in att_waits:
@@ -402,16 +427,15 @@
     for k in range(NX):
         mixed += dot(att_in[k], wall[k, pl.ds(1024, 128), :])
     normed = normalize([mixed], [gain2[...]])[0]
-    total_s = counts_f.at[pl.ds(0, 128), :]
-    total_s[...] = mixed
+    base_s[...] = mixed
 
     @pl.loop(0, NX)
     def _(k):
         hidden = dot(normed, wall[k, pl.ds(0, 512), :])
         hidden = (hidden * 0.5 * (1.0 + erf(hidden * 0.7071067811865476))).astype(BF16)
-        total_s[...] += dot(hidden, wall[k, pl.ds(512, 512), :])
-
-    out_ref[...] = total_s[...].astype(BF16)
+        base_s[...] += dot(hidden, wall[k, pl.ds(512, 512), :])
+
+    out_ref[...] = base_s[...].astype(BF16)
     net.finish()
 
 
@@ -419,8 +443,6 @@
          channel_logit_scaling, mixer_final_projector, neighbour_mixer_projector, expand_projector,
          contract_projector, matched_companion, boundary_sender_vertex, boundary_slot_tally,
          boundary_landing_vertex, partition_edge_tail, partition_edge_sink):
-    slot = jnp.arange(CAP, dtype=I32)
-    sender = jnp.where(slot[None, :] < boundary_slot_tally[0][:, None], boundary_sender_vertex[0], -1)
     vmem = pl.BlockSpec(memory_space=pltpu.VMEM)
     smem = pl.BlockSpec(memory_space=pltpu.SMEM)
     anywhere = pl.BlockSpec(memory_space=pl.ANY)
@@ -428,11 +450,12 @@
         kernel,
         name="layer",
         out_shape=jax.ShapeDtypeStruct((128, 512), BF16),
-        in_specs=[vmem, vmem, vmem, vmem, smem, anywhere, anywhere, anywhere, anywhere, smem, vmem, vmem, vmem, vmem],
+        in_specs=[vmem, vmem, vmem, vmem, smem, anywhere, anywhere, anywhere, anywhere, smem, vmem, smem, vmem, vmem, vmem],
         out_specs=vmem,
         scratch_shapes=[
             pltpu.VMEM((64, ROWS, LANES), BF16),
             pltpu.VMEM((NX, WROWS, 512), BF16),
+            pltpu.VMEM((NY, NZ, 1, 2 * CAP), I32),
             pltpu.VMEM((NZ, NY, 1, 2 * CAP), I32),
             pltpu.VMEM((NY, NZ, 1, 2 * CAP), I32),
             pltpu.VMEM((2, NY, NZ, 1, CAP), I32),
@@ -442,8 +465,7 @@
             pltpu.VMEM((NX, 128, ROWS), jnp.int16),
             pltpu.VMEM((ROWS, LANES), BF16),
             pltpu.VMEM((3, ROWS, LANES), BF16),
-            pltpu.VMEM((3, ROWS, LANES), BF16),
-            pltpu.VMEM((2, ROWS, LANES), F32),
+            pltpu.VMEM((2, 3, ROWS, LANES), BF16),
             pltpu.VMEM((2, ROWS, LANES), F32),
             pltpu.VMEM((2, ROWS, LANES), F32),
             pltpu.VMEM((ROWS, LANES), BF16),
@@ -469,7 +491,8 @@
         expand_projector,
         contract_projector,
         matched_companion,
-        sender.reshape(NY, NZ, 1, 2 * CAP),
+        boundary_sender_vertex.reshape(64, 1, CAP),
+        boundary_slot_tally,
         boundary_landing_vertex.reshape(64, 1, CAP),
         partition_edge_tail.reshape(128, LANES),
         partition_edge_sink.reshape(128, LANES),

time: 78.8 us -> 74.2 us (0.942)
  Pallas kernels: 74.2 us -> 72.5 us
  local copies, waits for them, and re-layouts: 2.96 us -> 1.57 us
  other arithmetic: 1.32 us -> 0 us
    pallas_call x1, Pallas kernels: 74.2 us -> 72.5 us  [body(): pl.pallas_call(kernel, name='layer', out_shape=jax.ShapeDtypeStruct((128,...]
    unnamed x6 -> x1, local copies, waits for them, and re-layouts: 2.77 us -> 1.57 us
where the time goes in v2:
time: 74.2 us; the launch traced here: 74.1 us
  Pallas kernels  72.5 us (98%)
  local copies, waits for them, and re-layouts  1.57 us (2%)
    pallas_call x1, Pallas kernels, body(): pl.pallas_call(kernel, name='layer', out_shape=jax.ShapeDtypeStruct((128,...  72.5 us
    unnamed x1, local copies, waits for them, and re-layouts  1.57 us

profile of v2, /device:TPU:1, one launch (start us, length us, event | category | flops | bytes accessed | tf_op | source)
XLA Modules:
  0.0 74.1 jit_solution(4662162063266490220)
XLA Ops:
  0.0 72.5 %layer.1 = bf16[128,512]{1,0:T(8,128)(2,1)} custom-call(bf16[512,512]{1,0:T(8,128)(2,1)} %x_ref.1, f32[1,512]{1,0:T(1,128)} %bitcast.11, f32[1,512]{1,0:T(1,128)} %bitcast.12, bf16[3,512,128]{2,1,0:T(8,128)(2,1)} %wqkv.1, f32[1,2]{1,0:T(1,128)} %bitcast.13, bf16[128,512]{1,0:T(8,128)(2,1)} %wf.1, bf16[128,512]{1,0:T(8,128)(2,1)} %wn.1, bf16[512,512]{1,0:T(8,128)(2,1)} %we.1, ...), custom_call_target="tpu_custom_call" | custom-call | tf_op jit(solution)/shard_map/layer/pallas_call | solution.py:449
  72.5 1.6 %copy.17 = bf16[128,512]{1,0:T(8,128)(2,1)} copy(bf16[128,512]{1,0:T(8,128)(2,1)} %layer.1) | data formatting | bytes 262144

commit v3 on v2

--- a/solution.py
+++ b/solution.py
@@ -15,7 +15,7 @@
 WROWS = 1280
 EPSILON = 1e-05
 LOG2E = 1.4426950408889634
-MESSAGES = 220
+MESSAGES = 127
 
 
 class Net:
@@ -89,7 +89,8 @@
         ring = NY if axis == "y" else NZ
         hy, hz = (sign, 0) if axis == "y" else (0, sign)
         if step == ring // 2:
-            low, high = half(low, high, sign)
+            if ((dz if axis == "y" else dy) + (1 if then == "z" else 0)) % 2 != (0 if sign > 0 else 1):
+                return
         oy, oz = dy - hy, dz - hz
         src = self.piece(net.dom(dy, dz), low, high)
         wait = net.send(src, src, net.at(hy, hz), self.piece(net.dom(oy, oz), low, high))
@@ -369,6 +370,7 @@
     for j in range(2):
         xp[j, m] = blocks[match_ref[j, net.me]]
     first_pair = exchange(0)
+    second_pair = exchange(1)
     for dz, t in ((3, 0), (2, 1), (4, 0), (3, 1), (4, 1)):
         land_pair(dz, t)
     for wait in ring_second:
@@ -376,7 +378,6 @@
     to_twin(2)
     for wait in first_pair:
         wait()
-    second_pair = exchange(1)
 
     final_waits = []
     for k in (2, 1, 3):

time: 74.2 us -> 70 us (0.943)
  Pallas kernels: 72.5 us -> 68.3 us
    pallas_call x1, Pallas kernels: 72.5 us -> 68.3 us  [body(): pl.pallas_call(kernel, name='layer', out_shape=jax.ShapeDtypeStruct((128,...]
where the time goes in v3:
time: 70 us; the launch traced here: 69.9 us
  Pallas kernels  68.3 us (98%)
  local copies, waits for them, and re-layouts  1.57 us (2%)
    pallas_call x1, Pallas kernels, body(): pl.pallas_call(kernel, name='layer', out_shape=jax.ShapeDtypeStruct((128,...  68.3 us
    unnamed x1, local copies, waits for them, and re-layouts  1.57 us

profile of v3, /device:TPU:1, one launch (start us, length us, event | category | flops | bytes accessed | tf_op | source)
XLA Modules:
  0.0 69.9 jit_solution(16473037942839145045)
XLA Ops:
  0.0 68.3 %layer.1 = bf16[128,512]{1,0:T(8,128)(2,1)} custom-call(bf16[512,512]{1,0:T(8,128)(2,1)} %x_ref.1, f32[1,512]{1,0:T(1,128)} %bitcast.11, f32[1,512]{1,0:T(1,128)} %bitcast.12, bf16[3,512,128]{2,1,0:T(8,128)(2,1)} %wqkv.1, f32[1,2]{1,0:T(1,128)} %bitcast.13, bf16[128,512]{1,0:T(8,128)(2,1)} %wf.1, bf16[128,512]{1,0:T(8,128)(2,1)} %wn.1, bf16[512,512]{1,0:T(8,128)(2,1)} %we.1, ...), custom_call_target="tpu_custom_call" | custom-call | tf_op jit(solution)/shard_map/layer/pallas_call | solution.py:450
  68.3 1.6 %copy.17 = bf16[128,512]{1,0:T(8,128)(2,1)} copy(bf16[128,512]{1,0:T(8,128)(2,1)} %layer.1) | data formatting | bytes 262144

commit v4 on v3

--- a/solution.py
+++ b/solution.py
@@ -16,6 +16,7 @@
 EPSILON = 1e-05
 LOG2E = 1.4426950408889634
 MESSAGES = 127
+POOL = 48
 
 
 class Net:
@@ -45,18 +46,20 @@
     def send(self, src, dst, device, landing):
         i = self.count
         self.count += 1
+        if i >= POOL:
+            self.open[i - POOL].wait_send()
         copy = pltpu.make_async_remote_copy(
-            src_ref=src, dst_ref=dst, send_sem=self.send_sems.at[i], recv_sem=self.recv_sems.at[i],
+            src_ref=src, dst_ref=dst, send_sem=self.send_sems.at[i % POOL], recv_sem=self.recv_sems.at[i],
             device_id=device, device_id_type=MESH)
         copy.start()
         self.open.append(copy)
         arrival = pltpu.make_async_remote_copy(
-            src_ref=landing, dst_ref=landing, send_sem=self.send_sems.at[i], recv_sem=self.recv_sems.at[i],
+            src_ref=landing, dst_ref=landing, send_sem=self.send_sems.at[i % POOL], recv_sem=self.recv_sems.at[i],
             device_id=device, device_id_type=MESH)
         return arrival.wait_recv
 
     def finish(self):
-        for copy in self.open:
+        for copy in self.open[-POOL:]:
             copy.wait_send()
 
 
@@ -475,7 +478,7 @@
             pltpu.VMEM((NX, 128, LANES), F32),
             pltpu.VMEM((ROWS, 2 * LANES), BF16),
             pltpu.VMEM((2, NX, ROWS, LANES), BF16),
-            pltpu.SemaphoreType.DMA((MESSAGES,)),
+            pltpu.SemaphoreType.DMA((POOL,)),
             pltpu.SemaphoreType.DMA((MESSAGES,)),
             pltpu.SemaphoreType.DMA((4,)),
         ],

time: 70 us -> 75 us (1.071)
  the two profiles are of different devices: /device:TPU:1 before, /device:TPU:6 now
where the time goes in v4:
time: 75 us; the launch traced here: 74.8 us
  Pallas kernels  73.2 us (98%)
  local copies, waits for them, and re-layouts  1.57 us (2%)
    pallas_call x1, Pallas kernels, body(): pl.pallas_call(kernel, name='layer', out_shape=jax.ShapeDtypeStruct((128,...  73.2 us
    unnamed x1, local copies, waits for them, and re-layouts  1.57 us

profile of v4, /device:TPU:6, one launch (start us, length us, event | category | flops | bytes accessed | tf_op | source)
XLA Modules:
  0.0 74.8 jit_solution(8465145657693779648)
XLA Ops:
  0.0 73.2 %layer.1 = bf16[128,512]{1,0:T(8,128)(2,1)} custom-call(bf16[512,512]{1,0:T(8,128)(2,1)} %x_ref.1, f32[1,512]{1,0:T(1,128)} %bitcast.11, f32[1,512]{1,0:T(1,128)} %bitcast.12, bf16[3,512,128]{2,1,0:T(8,128)(2,1)} %wqkv.1, f32[1,2]{1,0:T(1,128)} %bitcast.13, bf16[128,512]{1,0:T(8,128)(2,1)} %wf.1, bf16[128,512]{1,0:T(8,128)(2,1)} %wn.1, bf16[512,512]{1,0:T(8,128)(2,1)} %we.1, ...), custom_call_target="tpu_custom_call" | custom-call | tf_op jit(solution)/shard_map/layer/pallas_call | solution.py:453
  73.3 1.6 %copy.17 = bf16[128,512]{1,0:T(8,128)(2,1)} copy(bf16[128,512]{1,0:T(8,128)(2,1)} %layer.1) | data formatting | bytes 262144

commit v5 on v3

--- a/solution.py
+++ b/solution.py
@@ -373,21 +373,6 @@
     second_pair = exchange(1)
     for dz, t in ((3, 0), (2, 1), (4, 0), (3, 1), (4, 1)):
         land_pair(dz, t)
-    for wait in ring_second:
-        wait()
-    to_twin(2)
-    for wait in first_pair:
-        wait()
-
-    final_waits = []
-    for k in (2, 1, 3):
-        final_waits.append(net.send(bnd_s.at[rows128(net.ms[k]), pl.ds(0, LANES)], bnd_in.at[m],
-                                    net.along(k), bnd_in.at[net.ms[NX - k]]))
-    bnd_in[m] = bnd_s[own_rows, pl.ds(0, LANES)]
-
-    pair_project(0)
-    attend(1)
-
     for wait in count_waits:
         wait()
     total = (counts_in[0].astype(F32) + counts_in[1].astype(F32)
@@ -397,6 +382,21 @@
     base_s = counts_f.at[own_rows, :]
     degree = 1.0 + bnd_s[own_rows, pl.ds(LANES, 1)] + jnp.sum(total, -1, keepdims=True)
     base_s[...] = x_ref[own_rows, :].astype(F32) + dot(coarse, x_ref[...]) + dot(fine, x_ref[...])
+
+    for wait in ring_second:
+        wait()
+    to_twin(2)
+    for wait in first_pair:
+        wait()
+
+    final_waits = []
+    for k in (2, 1, 3):
+        final_waits.append(net.send(bnd_s.at[rows128(net.ms[k]), pl.ds(0, LANES)], bnd_in.at[m],
+                                    net.along(k), bnd_in.at[net.ms[NX - k]]))
+    bnd_in[m] = bnd_s[own_rows, pl.ds(0, LANES)]
+
+    pair_project(0)
+    attend(1)
 
     for wait in second_pair:
         wait()

time: 70 us -> 70 us (level)
  no operation moved by 1% of the time
where the time goes in v5:
time: 70 us; the launch traced here: 69.9 us
  Pallas kernels  68.3 us (98%)
  local copies, waits for them, and re-layouts  1.57 us (2%)
    pallas_call x1, Pallas kernels, body(): pl.pallas_call(kernel, name='layer', out_shape=jax.ShapeDtypeStruct((128,...  68.3 us
    unnamed x1, local copies, waits for them, and re-layouts  1.57 us

profile of v5, /device:TPU:1, one launch (start us, length us, event | category | flops | bytes accessed | tf_op | source)
XLA Modules:
  0.0 69.9 jit_solution(13067576416936831605)
XLA Ops:
  0.0 68.3 %layer.1 = bf16[128,512]{1,0:T(8,128)(2,1)} custom-call(bf16[512,512]{1,0:T(8,128)(2,1)} %x_ref.1, f32[1,512]{1,0:T(1,128)} %bitcast.11, f32[1,512]{1,0:T(1,128)} %bitcast.12, bf16[3,512,128]{2,1,0:T(8,128)(2,1)} %wqkv.1, f32[1,2]{1,0:T(1,128)} %bitcast.13, bf16[128,512]{1,0:T(8,128)(2,1)} %wf.1, bf16[128,512]{1,0:T(8,128)(2,1)} %wn.1, bf16[512,512]{1,0:T(8,128)(2,1)} %we.1, ...), custom_call_target="tpu_custom_call" | custom-call | tf_op jit(solution)/shard_map/layer/pallas_call | solution.py:450
  68.3 1.6 %copy.17 = bf16[128,512]{1,0:T(8,128)(2,1)} copy(bf16[128,512]{1,0:T(8,128)(2,1)} %layer.1) | data formatting | bytes 262144
